TPU v7x, 256 devices: a whole 4x4x8 slice. The times are simulated.
256 devices in a mesh: dp: 4 (over x), expert: 64 (over y, z, core).
Axes of the slice: x: 4, y: 4, z: 8, core: 2. Of those that a mesh axis runs over, the one named last changes fastest.
Arguments:
- tokens: bfloat16 [8192, 2048], P('expert'), may hold values from -4 to 4
- norm_gain: bfloat16 [2048], replicated, may hold values from 0.5 to 1.5
- routing_projection_matrix: bfloat16 [2048, 64], replicated, may hold values from -0.125 to 0.125
- experts: int32 [8192, 8], P('expert'), may hold values from 0 to 63, as said below
- replica_key: int32 [8192, 8], P('expert'), may hold values from 0 to 1048575
- slot_expert: int32 [128], replicated, may hold values from 0 to 63, as said below
- capacity: int32 [128], replicated, may hold values from 4 to 16, as said below
- slot_gate_up_weight: bfloat16 [128, 2048, 2, 1024], P('expert', None, None, 'dp'), may hold values from -0.125 to 0.125
- down_weight: bfloat16 [128, 1024, 2048], P('expert', 'dp'), may hold values from -0.1875 to 0.1875
Outputs:
- mixed: bfloat16 [8192, 2048], P('expert', 'dp')
Inputs may be any that keep to these rules, and one draw needn't show every extreme that they name: Each row names 8 different experts. `slot_expert`: every expert occupies at least one slot. `capacity`: for every j the capacities of slots 2 * j and 2 * j + 1 sum to at most 24, and to exactly 24 for some j.
All inputs are finite; a program needn't handle non-finite values.
Results may differ from a plain program's by a relative error of at most 0.012.
Values may be sent and summed in bfloat16 or wider, within the bound.
A program may use at most 128 MiB of HBM per device.

v0:
```python
import jax
import jax.numpy as jnp
from jax import lax
from jax.sharding import PartitionSpec as P

CAPACITY_HIGH = 16
CAP_DEV = 24


def assign_slots(experts, replica_key, slot_expert):
    flat_experts = experts.reshape(-1)
    holders = (flat_experts[:, None] == slot_expert[None, :]).astype(jnp.int32)
    copies = jnp.sum(holders, axis=1)
    earlier = jnp.cumsum(holders, axis=1) - holders
    wanted = replica_key.reshape(-1) % copies
    matched = holders * (earlier == wanted[:, None]).astype(jnp.int32)
    numbers = jnp.arange(slot_expert.shape[0], dtype=jnp.int32)
    return jnp.sum(matched * numbers[None, :], axis=1)


def slot_partial(flat_rows, gate_up_one, down_one):
    model_width = flat_rows.shape[1]
    unit_count = gate_up_one.shape[2]
    gate_up_out = jnp.dot(
        flat_rows,
        gate_up_one.reshape(model_width, 2 * unit_count),
        preferred_element_type=jnp.float32,
    )
    activated = (jax.nn.silu(gate_up_out[:, :unit_count]) * gate_up_out[:, unit_count:]).astype(
        jnp.bfloat16
    )
    result = jnp.dot(activated, down_one, preferred_element_type=jnp.float32)
    return result.astype(jnp.bfloat16)


def on_device(
    tokens,
    norm_gain,
    routing_projection_matrix,
    experts,
    replica_key,
    slot_expert,
    capacity,
    slot_gate_up_weight,
    down_weight,
):
    peer_count = lax.axis_size("expert")
    group_count = lax.axis_size("dp")
    group_pos = lax.axis_index("dp")
    me = lax.axis_index("expert")
    rows_here = tokens.shape[0]
    model_width = tokens.shape[1]
    pick_count = experts.shape[1]
    slot_count = slot_expert.shape[0]
    per_device = slot_count // peer_count
    quarter = model_width // group_count
    buffer_rows = CAP_DEV
    hidden = tokens.astype(jnp.float32)
    scale = lax.rsqrt(jnp.mean(hidden * hidden, axis=-1, keepdims=True) + 1e-06)
    normed = (hidden * scale * norm_gain.astype(jnp.float32)).astype(jnp.bfloat16)
    logits = jnp.dot(normed, routing_projection_matrix, preferred_element_type=jnp.float32)
    score = jax.nn.sigmoid(jnp.take_along_axis(logits, experts, axis=1)).reshape(-1)
    slot_ids = assign_slots(experts, replica_key, slot_expert)
    onehot = (slot_ids[:, None] == jnp.arange(slot_count, dtype=jnp.int32)[None, :]).astype(
        jnp.int32
    )
    position = jnp.sum((jnp.cumsum(onehot, axis=0) - onehot) * onehot, axis=1)
    slot_cap = jnp.sum(onehot * capacity[None, :], axis=1)
    kept_mask = position < slot_cap
    is_second = slot_ids % per_device == 1
    row_in = jnp.where(is_second, buffer_rows - slot_cap + position, position)
    target = jnp.where(
        kept_mask, slot_ids // per_device * buffer_rows + row_in, peer_count * buffer_rows
    )
    source_rows = jnp.arange(rows_here * pick_count, dtype=jnp.int32) // pick_count
    normed_part = lax.dynamic_slice_in_dim(normed, group_pos * quarter, quarter, 1)
    outgoing = (
        jnp.zeros((peer_count * buffer_rows + 1, quarter), jnp.bfloat16)
        .at[target]
        .set(normed_part[source_rows])
    )
    outgoing = outgoing[:-1].reshape(peer_count, buffer_rows, quarter)
    incoming_part = lax.all_to_all(outgoing, "expert", split_axis=0, concat_axis=0, tiled=True)
    incoming = lax.all_gather(incoming_part, "dp", axis=2, tiled=True)
    flat_in = incoming.reshape(peer_count * buffer_rows, model_width)
    first_out = slot_partial(flat_in, slot_gate_up_weight[0], down_weight[0])
    second_out = slot_partial(flat_in, slot_gate_up_weight[1], down_weight[1])
    first_cap = lax.dynamic_index_in_dim(capacity, me * per_device, keepdims=False)
    row_index = jnp.arange(peer_count * buffer_rows, dtype=jnp.int32) % buffer_rows
    partial_value = jnp.where((row_index < first_cap)[:, None], first_out, second_out)
    partial_value = partial_value.reshape(peer_count, buffer_rows, model_width)
    summed = lax.psum_scatter(partial_value, "dp", scatter_dimension=2, tiled=True)
    returned = lax.all_to_all(summed, "expert", split_axis=0, concat_axis=0, tiled=True)
    flat_ret = returned.reshape(peer_count * buffer_rows, quarter)
    flat_ret = jnp.concatenate([flat_ret, jnp.zeros((1, quarter), flat_ret.dtype)])
    weight_kept = jnp.where(kept_mask, score, jnp.float32(0.0))
    gathered = flat_ret[target].astype(jnp.float32).reshape(rows_here, pick_count, quarter)
    mixture = jnp.sum(weight_kept.reshape(rows_here, pick_count)[:, :, None] * gathered, axis=1)
    residual = lax.dynamic_slice_in_dim(tokens, group_pos * quarter, quarter, 1).astype(jnp.float32)
    return (residual + mixture).astype(jnp.bfloat16)


def solution(mesh):
    in_specs = (
        P("expert", None),
        P(),
        P(),
        P("expert", None),
        P("expert", None),
        P(),
        P(),
        P("expert", None, None, "dp"),
        P("expert", "dp", None),
    )
    out_specs = P("expert", "dp")
    return jax.shard_map(
        on_device, mesh=mesh, in_specs=in_specs, out_specs=out_specs, check_vma=False
    )
```

profile of v0, /device:TPU:1, one launch (start us, length us, event | category | flops | bytes accessed | tf_op | source)
XLA Modules:
  0.0 289.3 jit_solution(4413022350040989855)
XLA Ops:
  6.6 0.8 copy.21
  7.4 0.1 eq.65
  7.5 0.8 convert_reduce_fusion
  8.3 0.8 compare_convert_fusion
  9.0 1.2 fusion.3
  10.3 0.7 convert_element_type.50
  11.0 0.8 copy.22
  11.8 0.1 reshape.250
  11.9 0.5 reduce_window_sum.26
  12.4 0.1 add_select_fusion.1
  12.5 0.2 fusion.19
  12.7 0.1 copy.23
  12.8 0.2 fusion.23
  13.1 0.3 copy.24
  13.4 0.2 fusion.5
  13.6 0.2 select_reduce_fusion
  13.9 0.5 copy-done.2
  14.4 10.1 %scatter_custom_fusion = bf16[1537,512]{1,0:T(8,128)(2,1)S(1)} fusion(s32[1024]{0:T(1024)S(1)} %bitcast.69, bf16[128,512]{1,0:T(8,128)(2,1)S(1)} %constant_dynamic-slice_fusion, s32[1024]{0:T(1024)S(1)} %broadcast_clamp_fusion.1, bf16[]{:T(256)} %constant.114.clone.1), kind=kCustom, calls=%fused_computation.20 | custom fusion | bytes 1573890 | tf_op jit(solution)/shard_map/scatter | solution.py:80
  24.5 0.1 slice.52
  24.6 52.9 %all_to_all.10 = bf16[64,24,512]{2,1,0:T(8,128)(2,1)} all-to-all(bf16[64,24,512]{2,1,0:T(8,128)(2,1)S(1)} %bitcast.59), channel_id=1, replica_groups=mesh['dp'=4,'expert'=64] {'expert'}, dimensions={0} | all-to-all | bytes 3145728 | tf_op jit(solution)/shard_map/all_to_all | solution.py:83
  77.5 0.0 all-gather.2.cloned.1.call-update
  77.5 0.2 reduce-scatter.2.cloned.1.call-start
  77.7 0.6 dynamic_slice.11
  78.3 4.7 %fusion.32 = (bf16[1,2048,2,256]{3,2,1,0:T(2,128)(2,1)S(1)}, bf16[1,2048,2,256]{3,2,1,0:T(2,128)(2,1)S(1)}) fusion(bf16[2,2048,2,256]{3,2,1,0:T(2,128)(2,1)} %param.16), kind=kLoop, calls=%fused_computation.77 | loop fusion | bytes 8388608 | tf_op jit(solution)/shard_map/slice | solution.py:86
  83.0 0.5 copy.30
  83.5 1.8 copy.31
  85.4 0.7 fusion.26
  86.0 56.6 %all-gather.2.cloned.1.call-done = bf16[64,24,2048]{2,1,0:T(8,128)(2,1)} async-done(((bf16[64,24,512]{2,1,0:T(8,128)(2,1)}), bf16[64,24,2048]{2,1,0:T(8,128)(2,1)}) %all-gather.2.cloned.1.call-update) | async-done | bytes 6291472 | tf_op jit(solution)/shard_map/all_gather | solution.py:84
  142.6 6.3 %fusion.35 = f32[1536,512]{1,0:T(8,128)S(1)} fusion(bf16[1536,2048]{1,0:T(8,128)(2,1)} %bitcast.71, bf16[2048,512]{1,0:T(8,128)(2,1)} %bitcast.62), kind=kOutput, calls=%fused_computation.80 | convolution fusion | flops 3221225472 | bytes 11534336 | tf_op jit(solution)/shard_map/dot_general | solution.py:24
  148.9 3.5 %fusion.34 = f32[1536,512]{1,0:T(8,128)S(1)} fusion(bf16[1536,2048]{1,0:T(8,128)(2,1)S(1)} %bitcast.72, bf16[2048,512]{1,0:T(8,128)(2,1)S(1)} %bitcast.61), kind=kOutput, calls=%fused_computation.79 | convolution fusion | flops 3221225472 | bytes 11534336 | tf_op jit(solution)/shard_map/dot_general | solution.py:24
  152.4 1.9 convolution_convert_fusion
  154.3 3.9 %broadcast_select_fusion = bf16[1536,2048]{1,0:T(8,128)(2,1)} fusion(bf16[1536,2048]{1,0:T(8,128)(2,1)S(1)} %convolution_convert_fusion, pred[1536]{0:T(1024)(128)(4,1)S(1)} %fusion.26, bf16[2,256,2048]{2,1,0:T(8,128)(2,1)S(1)} %copy-done.8, f32[1536,512]{1,0:T(8,128)S(1)} %fusion.34), kind=kOutput, calls=%fused_computation.6 | convolution fusion | flops 1619263488 | bytes 16779264 | tf_op jit(solution)/shard_map/dot_general | solution.py:32
  158.2 0.0 reduce-scatter.2.cloned.1.call-update
  158.3 67.4 %reduce-scatter.2.cloned.1.call-done = bf16[64,24,512]{2,1,0:T(8,128)(2,1)} async-done(((bf16[64,24,2048]{2,1,0:T(8,128)(2,1)}), bf16[64,24,512]{2,1,0:T(8,128)(2,1)}) %reduce-scatter.2.cloned.1.call-update) | async-done | bytes 1572880 | tf_op jit(solution)/shard_map/reduce_scatter | solution.py:92
  225.7 10.6 %all-to-all-start.1 = ((bf16[64,24,512]{2,1,0:T(8,128)(2,1)}), bf16[64,24,512]{2,1,0:T(8,128)(2,1)S(1)}, u32[]{:S(2)}, u32[]{:S(2)}) async-start(bf16[64,24,512]{2,1,0:T(8,128)(2,1)} %reduce-scatter.2.cloned.1.call-done), calls=%async_computation.2 | async-start | bytes 3145728 | tf_op jit(solution)/shard_map/all_to_all | solution.py:93
  236.3 0.1 copy.25
  236.5 0.1 reshape.274
  236.6 0.3 fusion.33
  236.9 7.0 %gather_fusion.1 = f32[1024]{0:T(1024)S(1)} fusion(f32[128,64]{0,1:T(8,128)S(1)} %fusion.33, s32[1024]{0:T(1024)S(1)} %reshape.274), kind=kCustom, calls=%fused_computation.2 | custom fusion | bytes 16384 | tf_op jit(solution)/shard_map/jit(take_along_axis)/gather | solution.py:62
  243.9 0.1 reshape.277
  244.0 0.1 lt.96
  244.2 0.1 copy.27
  244.3 0.1 copy.28
  244.4 31.7 %all-to-all-done.1 = bf16[64,24,512]{2,1,0:T(8,128)(2,1)S(1)} async-done(((bf16[64,24,512]{2,1,0:T(8,128)(2,1)}), bf16[64,24,512]{2,1,0:T(8,128)(2,1)S(1)}, u32[]{:S(2)}, u32[]{:S(2)}) %all-to-all-start.1) | async-done | bytes 1572896 | tf_op jit(solution)/shard_map/all_to_all | solution.py:93
  276.1 0.1 concatenate.3
  276.2 4.0 %gather_fusion = bf16[1024,512]{1,0:T(8,128)(2,1)S(1)} fusion(bf16[1537,512]{1,0:T(8,128)(2,1)S(1)} %concatenate.3, s32[1024]{0:T(1024)S(1)} %broadcast_clamp_fusion), kind=kCustom, calls=%fused_computation.1 | custom fusion | bytes 2101248 | tf_op jit(solution)/shard_map/gather | solution.py:97
  280.2 0.7 fusion
  280.9 1.6 add_convert_fusion
  (32 shorter events, 0.3 us)
Async XLA Ops:
  6.5 230.0 %copy-start = (bf16[2048,64]{0,1:T(8,128)(2,1)S(1)}, bf16[2048,64]{0,1:T(8,128)(2,1)}, u32[]{:S(2)}) copy-start(bf16[2048,64]{0,1:T(8,128)(2,1)} %param.11) | copy-start | bytes 786436
  6.5 5.9 %copy-start.5 = (s32[128]{0:T(128)S(1)}, s32[128]{0:T(128)}, u32[]{:S(2)}) copy-start(s32[128]{0:T(128)} %param.14) | copy-start | bytes 1540
  6.5 136.1 %all-gather.2.cloned.1.call-start = ((), (), s32[]{:S(2)}) async-start(), calls=%async_computation.3 | async-start | bytes 7864320 | tf_op jit(solution)/shard_map/all_gather | solution.py:84
  11.9 1.5 copy-start.1
  12.7 0.9 copy-start.6
  13.6 0.8 copy-start.2
  77.5 148.1 %reduce-scatter.2.cloned.1.call-start = ((), (), s32[]{:S(2)}) async-start(), calls=%async_computation.4 | async-start | bytes 7864320 | tf_op jit(solution)/shard_map/reduce_scatter | solution.py:92
  142.6 6.3 %copy-start.7 = (bf16[64,24,2048]{2,1,0:T(8,128)(2,1)S(1)}, bf16[64,24,2048]{2,1,0:T(8,128)(2,1)}, u32[]{:S(2)}) copy-start(bf16[64,24,2048]{2,1,0:T(8,128)(2,1)} %all-gather.2.cloned.1.call-done) | copy-start | bytes 18874372
  148.9 3.5 %copy-start.8 = (bf16[2,256,2048]{2,1,0:T(8,128)(2,1)S(1)}, bf16[2,256,2048]{2,1,0:T(8,128)(2,1)}, u32[]{:S(2)}) copy-start(bf16[2,256,2048]{2,1,0:T(8,128)(2,1)} %param.17) | copy-start | bytes 6291460
  158.2 78.1 %copy-start.4 = (s32[128,8]{0,1:T(8,128)S(1)}, s32[128,8]{0,1:T(8,128)}, u32[]{:S(2)}) copy-start(s32[128,8]{0,1:T(8,128)} %param.12) | copy-start | bytes 12292
  158.3 78.3 %copy-start.3 = (bf16[128,2048]{1,0:T(8,128)(2,1)S(1)}, bf16[128,2048]{1,0:T(8,128)(2,1)}, u32[]{:S(2)}) copy-start(bf16[128,2048]{1,0:T(8,128)(2,1)} %copy-done.2) | copy-start | bytes 1572868
  225.7 50.4 %all-to-all-start.1 = ((bf16[64,24,512]{2,1,0:T(8,128)(2,1)}), bf16[64,24,512]{2,1,0:T(8,128)(2,1)S(1)}, u32[]{:S(2)}, u32[]{:S(2)}) async-start(bf16[64,24,512]{2,1,0:T(8,128)(2,1)} %reduce-scatter.2.cloned.1.call-done), calls=%async_computation.2 | async-start | bytes 3145728 | tf_op jit(solution)/shard_map/all_to_all | solution.py:93
Sparse Core Ops, SparseCore 0:
  77.6 64.9 all-gather.1
  158.4 67.2 reduce-scatter.1
where the time goes:
time: 290 us; the launch traced here: 289 us
  waiting for transfers between devices  156 us (54%)
  blocking collectives  52.9 us (18%)
  local copies, waits for them, and re-layouts  32.3 us (11%)
  matrix products  15.8 us (5%)
  between operations  13.8 us (5%)
  starting transfers between devices  10.9 us (4%)
  other arithmetic  7.97 us (3%)
    reduce_scatter x1, waiting for transfers between devices, on_device(): lax.psum_scatter(partial_value, 'dp', scatter_dimension=2, tiled=True)  67.4 us
    all_gather x1, waiting for transfers between devices, on_device(): incoming = lax.all_gather(incoming_part, 'dp', axis=2, tiled=True)  56.6 us
    all_to_all x1, blocking collectives, on_device(): lax.all_to_all(outgoing, 'expert', split_axis=0, concat_axis=0, tiled=True)  52.9 us
    all_to_all x1, waiting for transfers between devices, on_device(): lax.all_to_all(summed, 'expert', split_axis=0, concat_axis=0, tiled=True)  31.7 us
    all_to_all x1, starting transfers between devices, on_device(): lax.all_to_all(summed, 'expert', split_axis=0, concat_axis=0, tiled=True)  10.6 us
    scatter x1, local copies, waits for them, and re-layouts, on_device(): outgoing = jnp.zeros((peer_count * buffer_rows + 1, quarter), jnp.bfloat1...  10.1 us
    dot_general x2, matrix products, slot_partial(): jnp.dot(flat_rows, gate_up_one.reshape(model_width, 2 * unit_count), pref...  9.76 us
    gather x5, local copies, waits for them, and re-layouts, on_device(): jnp.take_along_axis(logits, experts, axis=1)  7.34 us
  transfers between devices with their start and end apart: 3, of which 3 were waited for; matrix products, arithmetic and copies ran while one was open for 6% of the time, Pallas kernels for 0%

commit v1 on v0

--- a/solution.py
+++ b/solution.py
@@ -5,6 +5,12 @@
 
 CAPACITY_HIGH = 16
 CAP_DEV = 24
+
+
+def gather_by_exchange(x, axis, dim):
+    count = lax.axis_size(axis)
+    repeats = [count if d == dim else 1 for d in range(x.ndim)]
+    return lax.all_to_all(jnp.tile(x, repeats), axis, split_axis=dim, concat_axis=dim, tiled=True)
 
 
 def assign_slots(experts, replica_key, slot_expert):
@@ -81,7 +87,7 @@
     )
     outgoing = outgoing[:-1].reshape(peer_count, buffer_rows, quarter)
     incoming_part = lax.all_to_all(outgoing, "expert", split_axis=0, concat_axis=0, tiled=True)
-    incoming = lax.all_gather(incoming_part, "dp", axis=2, tiled=True)
+    incoming = gather_by_exchange(incoming_part, "dp", 2)
     flat_in = incoming.reshape(peer_count * buffer_rows, model_width)
     first_out = slot_partial(flat_in, slot_gate_up_weight[0], down_weight[0])
     second_out = slot_partial(flat_in, slot_gate_up_weight[1], down_weight[1])

time: 290 us -> 349 us (1.20)
  local copies, waits for them, and re-layouts: 32.3 us -> 86.2 us
  starting transfers between devices: 10.9 us -> 15.9 us
    all_to_all x0 -> x1, waiting for transfers between devices: none -> 62.9 us  [gather_by_exchange(): lax.all_to_all(jnp.tile(x, repeats), axis, split_axis=dim, concat_axis=di...]
    all_gather x1 -> x0, waiting for transfers between devices: 56.6 us -> none  [on_device(): incoming = lax.all_gather(incoming_part, 'dp', axis=2, tiled=True)]
    unnamed x22 -> x26, local copies, waits for them, and re-layouts: 4.48 us -> 30.3 us
    all_to_all x0 -> x2, local copies, waits for them, and re-layouts: none -> 22 us  [the longest x1 17.2 us: gather_by_exchange(): lax.all_to_all(jnp.tile(x, repeats), axis, split_axis=dim, concat_axis=di...]
    another operation x3 -> x4, local copies, waits for them, and re-layouts: 0.28 us -> 6.46 us  [the longest x1 6.19 us: gather_by_exchange(): jnp.tile(x, repeats)]
    reduce_scatter x1, waiting for transfers between devices: 67.4 us -> 61.9 us  [on_device(): lax.psum_scatter(partial_value, 'dp', scatter_dimension=2, tiled=True)]
    all_to_all x0 -> x1, starting transfers between devices: none -> 5.28 us  [gather_by_exchange(): lax.all_to_all(jnp.tile(x, repeats), axis, split_axis=dim, concat_axis=di...]
  transfers between devices with their start and end apart: 3 -> 3, of which waited for: 3 -> 3; matrix products, arithmetic and copies ran while one was open for 6% -> 5% of each run, Pallas kernels for 0% -> 0%
where the time goes in v1:
time: 349 us; the launch traced here: 348 us
  waiting for transfers between devices  157 us (45%)
  local copies, waits for them, and re-layouts  86.2 us (25%)
  blocking collectives  52.9 us (15%)
  starting transfers between devices  15.9 us (5%)
  matrix products  15.7 us (4%)
  between operations  13.8 us (4%)
  other arithmetic  6.91 us (2%)
    all_to_all x1, waiting for transfers between devices, gather_by_exchange(): lax.all_to_all(jnp.tile(x, repeats), axis, split_axis=dim, concat_axis=di...  62.9 us
    reduce_scatter x1, waiting for transfers between devices, on_device(): lax.psum_scatter(partial_value, 'dp', scatter_dimension=2, tiled=True)  61.9 us
    all_to_all x1, blocking collectives, on_device(): lax.all_to_all(outgoing, 'expert', split_axis=0, concat_axis=0, tiled=True)  52.9 us
    all_to_all x1, waiting for transfers between devices, on_device(): lax.all_to_all(summed, 'expert', split_axis=0, concat_axis=0, tiled=True)  31.7 us
    unnamed x26, local copies, waits for them, and re-layouts  30.3 us
    all_to_all x1, local copies, waits for them, and re-layouts, gather_by_exchange(): lax.all_to_all(jnp.tile(x, repeats), axis, split_axis=dim, concat_axis=di...  17.2 us
    all_to_all x1, starting transfers between devices, on_device(): lax.all_to_all(summed, 'expert', split_axis=0, concat_axis=0, tiled=True)  10.6 us
    scatter x1, local copies, waits for them, and re-layouts, on_device(): outgoing = jnp.zeros((peer_count * buffer_rows + 1, quarter), jnp.bfloat1...  10.1 us
  transfers between devices with their start and end apart: 3, of which 3 were waited for; matrix products, arithmetic and copies ran while one was open for 5% of the time, Pallas kernels for 0%

profile of v1, /device:TPU:1, one launch (start us, length us, event | category | flops | bytes accessed | tf_op | source)
XLA Modules:
  0.0 348.0 jit_solution(16013226307849434911)
XLA Ops:
  6.5 0.8 copy.52
  7.4 0.1 eq.65
  7.5 0.8 compare_convert_fusion
  8.2 0.8 convert_reduce_fusion
  9.0 0.8 copy.53
  9.8 0.1 reshape.254
  9.9 0.5 reduce_window_sum.26
  10.4 0.1 add_select_fusion.1
  10.6 0.9 fusion.19
  11.4 0.1 copy.54
  11.5 0.2 fusion.23
  11.8 0.3 copy.55
  12.1 0.2 fusion.3
  12.3 0.2 select_reduce_fusion
  12.5 0.2 fusion.5
  12.8 0.7 copy-done.3
  13.6 10.1 %scatter_custom_fusion = bf16[1537,512]{1,0:T(8,128)(2,1)S(1)} fusion(s32[1024]{0:T(1024)S(1)} %bitcast.75, bf16[128,512]{1,0:T(8,128)(2,1)S(1)} %constant_dynamic-slice_fusion, s32[1024]{0:T(1024)S(1)} %broadcast_clamp_fusion.1, bf16[]{:T(256)} %constant.114.clone.1), kind=kCustom, calls=%fused_computation.20 | custom fusion | bytes 1573890 | tf_op jit(solution)/shard_map/scatter | solution.py:86
  23.7 0.1 slice.52
  23.8 52.9 %all_to_all.15 = bf16[64,24,512]{2,1,0:T(8,128)(2,1)} all-to-all(bf16[64,24,512]{2,1,0:T(8,128)(2,1)S(1)} %bitcast.63), channel_id=1, replica_groups=mesh['dp'=4,'expert'=64] {'expert'}, dimensions={0} | all-to-all | bytes 3145728 | tf_op jit(solution)/shard_map/all_to_all | solution.py:89
  76.7 4.8 %copy.60 = bf16[64,24,512]{0,1,2:T(8,128)(2,1)S(1)} copy(bf16[64,24,512]{2,1,0:T(8,128)(2,1)} %all_to_all.15) | data formatting | bytes 3145728 | tf_op jit(solution)/shard_map/all_to_all | solution.py:89
  81.5 6.2 %tile.4 = bf16[64,24,4,512]{0,1,3,2:T(8,128)(2,1)} broadcast(bf16[64,24,512]{0,1,2:T(8,128)(2,1)S(1)} %copy.60), dimensions={0,1,3} | broadcast | bytes 7864320 | tf_op jit(solution)/shard_map/tile | solution.py:13
  87.7 12.8 %reshape.303 = bf16[4,2,393216]{2,1,0:T(2,128)(2,1)} reshape(bf16[2048,24,64]{2,1,0:T(8,128)(2,1)} %bitcast.59) | data formatting | bytes 12582912
  100.5 5.3 %all-to-all-start.1 = ((bf16[4,2,393216]{2,1,0:T(2,128)(2,1)}), bf16[4,2,393216]{2,1,0:T(2,128)(2,1)}, u32[]{:S(2)}, u32[]{:S(2)}) async-start(bf16[4,2,393216]{2,1,0:T(2,128)(2,1)} %reshape.303), calls=%async_computation.1 | async-start | bytes 12582912 | tf_op jit(solution)/shard_map/all_to_all | solution.py:13
  105.9 4.7 %fusion.32 = (bf16[1,2048,2,256]{3,2,1,0:T(2,128)(2,1)S(1)}, bf16[1,2048,2,256]{3,2,1,0:T(2,128)(2,1)S(1)}) fusion(bf16[2,2048,2,256]{3,2,1,0:T(2,128)(2,1)} %param.16), kind=kLoop, calls=%fused_computation.77 | loop fusion | bytes 8388608 | tf_op jit(solution)/shard_map/slice | solution.py:92
  110.5 0.5 copy.64
  111.1 1.9 copy.63
  113.0 0.6 dynamic_slice.11
  113.6 0.7 fusion.26
  114.2 62.9 %all-to-all-done.1 = bf16[4,2,393216]{2,1,0:T(2,128)(2,1)} async-done(((bf16[4,2,393216]{2,1,0:T(2,128)(2,1)}), bf16[4,2,393216]{2,1,0:T(2,128)(2,1)}, u32[]{:S(2)}, u32[]{:S(2)}) %all-to-all-start.1) | async-done | bytes 6291488 | tf_op jit(solution)/shard_map/all_to_all | solution.py:13
  177.1 12.6 %reshape.304 = bf16[2048,24,64]{2,1,0:T(8,128)(2,1)} reshape(bf16[4,2,393216]{2,1,0:T(2,128)(2,1)} %all-to-all-done.1) | data formatting | bytes 12582912
  189.8 17.2 %copy.61 = bf16[64,24,2048]{2,1,0:T(8,128)(2,1)} copy(bf16[64,24,2048]{0,1,2:T(8,128)(2,1)} %bitcast.58) | data formatting | bytes 12582912 | tf_op jit(solution)/shard_map/all_to_all | solution.py:13
  206.9 6.1 %fusion.35 = f32[1536,512]{1,0:T(8,128)S(1)} fusion(bf16[1536,2048]{1,0:T(8,128)(2,1)} %bitcast.65, bf16[2048,512]{1,0:T(8,128)(2,1)S(1)} %bitcast.67), kind=kOutput, calls=%fused_computation.80 | convolution fusion | flops 3221225472 | bytes 11534336 | tf_op jit(solution)/shard_map/dot_general | solution.py:30
  213.1 3.5 fusion.34
  216.5 1.9 convolution_convert_fusion
  218.4 4.0 %broadcast_select_fusion = bf16[1536,2048]{1,0:T(8,128)(2,1)} fusion(bf16[1536,2048]{1,0:T(8,128)(2,1)S(1)} %convolution_convert_fusion, pred[1536]{0:T(1024)(128)(4,1)S(1)} %fusion.26, bf16[2,256,2048]{2,1,0:T(8,128)(2,1)S(1)} %copy-done.9, f32[1536,512]{1,0:T(8,128)S(1)} %fusion.34), kind=kOutput, calls=%fused_computation.6 | convolution fusion | flops 1619263488 | bytes 16779264 | tf_op jit(solution)/shard_map/dot_general | solution.py:38
  222.5 61.9 %reduce-scatter.2.cloned.1.call-done = bf16[64,24,512]{2,1,0:T(8,128)(2,1)} async-done(((bf16[64,24,2048]{2,1,0:T(8,128)(2,1)}), bf16[64,24,512]{2,1,0:T(8,128)(2,1)}) %reduce-scatter.2.cloned.1.call-update) | async-done | bytes 1572880 | tf_op jit(solution)/shard_map/reduce_scatter | solution.py:98
  284.4 10.6 %all-to-all-start.2 = ((bf16[64,24,512]{2,1,0:T(8,128)(2,1)}), bf16[64,24,512]{2,1,0:T(8,128)(2,1)S(1)}, u32[]{:S(2)}, u32[]{:S(2)}) async-start(bf16[64,24,512]{2,1,0:T(8,128)(2,1)} %reduce-scatter.2.cloned.1.call-done), calls=%async_computation.3 | async-start | bytes 3145728 | tf_op jit(solution)/shard_map/all_to_all | solution.py:99
  295.0 0.1 lt.96
  295.2 0.1 copy.56
  295.3 0.1 reshape.278
  295.4 0.3 fusion.33
  295.7 7.0 %gather_fusion.1 = f32[1024]{0:T(1024)S(1)} fusion(f32[128,64]{0,1:T(8,128)S(1)} %fusion.33, s32[1024]{0:T(1024)S(1)} %reshape.278), kind=kCustom, calls=%fused_computation.2 | custom fusion | bytes 16384 | tf_op jit(solution)/shard_map/jit(take_along_axis)/gather | solution.py:68
  302.9 0.1 copy.59
  303.1 31.7 %all-to-all-done.2 = bf16[64,24,512]{2,1,0:T(8,128)(2,1)S(1)} async-done(((bf16[64,24,512]{2,1,0:T(8,128)(2,1)}), bf16[64,24,512]{2,1,0:T(8,128)(2,1)S(1)}, u32[]{:S(2)}, u32[]{:S(2)}) %all-to-all-start.2) | async-done | bytes 1572896 | tf_op jit(solution)/shard_map/all_to_all | solution.py:99
  334.8 0.1 concatenate.3
  334.9 4.0 %gather_fusion = bf16[1024,512]{1,0:T(8,128)(2,1)S(1)} fusion(bf16[1537,512]{1,0:T(8,128)(2,1)S(1)} %concatenate.3, s32[1024]{0:T(1024)S(1)} %broadcast_clamp_fusion), kind=kCustom, calls=%fused_computation.1 | custom fusion | bytes 2101248 | tf_op jit(solution)/shard_map/gather | solution.py:103
  338.9 0.7 fusion
  339.6 1.6 add_convert_fusion
  (38 shorter events, 0.5 us)
Async XLA Ops:
  6.5 288.9 %copy-start = (bf16[2048,64]{0,1:T(8,128)(2,1)S(1)}, bf16[2048,64]{0,1:T(8,128)(2,1)}, u32[]{:S(2)}) copy-start(bf16[2048,64]{0,1:T(8,128)(2,1)} %param.11) | copy-start | bytes 786436
  9.9 2.2 copy-start.7
  9.9 2.2 copy-start.2
  10.4 1.9 copy-start.8
  12.7 0.8 copy-start.3
  100.5 76.6 %all-to-all-start.1 = ((bf16[4,2,393216]{2,1,0:T(2,128)(2,1)}), bf16[4,2,393216]{2,1,0:T(2,128)(2,1)}, u32[]{:S(2)}, u32[]{:S(2)}) async-start(bf16[4,2,393216]{2,1,0:T(2,128)(2,1)} %reshape.303), calls=%async_computation.1 | async-start | bytes 12582912 | tf_op jit(solution)/shard_map/all_to_all | solution.py:13
  105.8 178.6 %reduce-scatter.2.cloned.1.call-start = ((), (), s32[]{:S(2)}) async-start(), calls=%async_computation.4 | async-start | bytes 7864320 | tf_op jit(solution)/shard_map/reduce_scatter | solution.py:98
  206.9 6.1 %copy-start.1 = (bf16[64,24,2048]{2,1,0:T(8,128)(2,1)S(1)}, bf16[64,24,2048]{2,1,0:T(8,128)(2,1)}, u32[]{:S(2)}) copy-start(bf16[64,24,2048]{2,1,0:T(8,128)(2,1)} %copy.61) | copy-start | bytes 18874372
  206.9 6.1 %copy-start.5 = (bf16[256,8,2,256]{3,1,2,0:T(8,128)(2,1)S(1)}, bf16[256,8,2,256]{3,1,2,0:T(8,128)(2,1)}, u32[]{:S(2)}) copy-start(bf16[256,8,2,256]{3,1,2,0:T(8,128)(2,1)} %copy.63) | copy-start | bytes 6291460
  213.1 3.5 copy-start.9
  222.4 72.7 %copy-start.6 = (s32[128,8]{0,1:T(8,128)S(1)}, s32[128,8]{0,1:T(8,128)}, u32[]{:S(2)}) copy-start(s32[128,8]{0,1:T(8,128)} %param.12) | copy-start | bytes 12292
  222.5 73.0 %copy-start.4 = (bf16[128,2048]{1,0:T(8,128)(2,1)S(1)}, bf16[128,2048]{1,0:T(8,128)(2,1)}, u32[]{:S(2)}) copy-start(bf16[128,2048]{1,0:T(8,128)(2,1)} %copy-done.3) | copy-start | bytes 1572868
  284.4 50.4 %all-to-all-start.2 = ((bf16[64,24,512]{2,1,0:T(8,128)(2,1)}), bf16[64,24,512]{2,1,0:T(8,128)(2,1)S(1)}, u32[]{:S(2)}, u32[]{:S(2)}) async-start(bf16[64,24,512]{2,1,0:T(8,128)(2,1)} %reduce-scatter.2.cloned.1.call-done), calls=%async_computation.3 | async-start | bytes 3145728 | tf_op jit(solution)/shard_map/all_to_all | solution.py:99
Sparse Core Ops, SparseCore 0:
  222.6 61.7 reduce-scatter.1
